TPU v7x, 512 devices: a whole 4x4x16 slice. The times are simulated.
512 devices in a mesh: seq: 32 (over z, core), dp: 16 (over y, x).
Axes of the slice: x: 4, y: 4, z: 16, core: 2. Of those that a mesh axis runs over, the one named last changes fastest.
Arguments:
- queries: bfloat16 [16, 4096, 1024], P('dp', 'seq'), may hold values from -6 to 6
- key_vectors: bfloat16 [16, 4096, 1024], P('dp', 'seq'), may hold values from -6 to 6
- value_vectors: bfloat16 [16, 4096, 1024], P('dp', 'seq'), may hold values from -64 to 64
- log_decay: float32 [16, 4096, 16], P('dp', 'seq'), may hold values from -1 to 0, as said below
- restart: int32 [16, 4096], P('dp', 'seq'), may hold values 0 or 1
- norm_gain: float32 [1024], replicated, may hold values from 0.5 to 1.5
- upstream: bfloat16 [16, 4096, 1024], P('dp', 'seq'), may hold values from -6 to 6
Outputs:
- layer_out: bfloat16 [16, 4096, 1024], P('dp', 'seq')
- grad_query: bfloat16 [16, 4096, 1024], P('dp', 'seq')
- grad_key: bfloat16 [16, 4096, 1024], P('dp', 'seq')
- grad_value: bfloat16 [16, 4096, 1024], P('dp', 'seq')
- grad_decay: float32 [16, 4096, 16], P('dp', 'seq')
- grad_gain: float32 [1024], replicated
Inputs may be any that keep to these rules, and one draw needn't show every extreme that they name: `log_decay`: never positive. `restart`: 1 marks a sample before which the state is cleared.
All inputs are finite; a program needn't handle non-finite values. No bound on the sum of `restart` on one device may be relied on, other than what follows from the above.
Results may differ from a plain program's by a relative error of at most 0.0096.
Values sent between devices are 32-bit elements; how exact they have to be, the bound alone decides.
A program may use at most 128 MiB of HBM per device.

v0:
```python
import jax
import jax.numpy as jnp
from jax import lax
from jax.sharding import PartitionSpec as P

HEAD_TOTAL = 16


EPSILON = 1e-06
EXACT = lax.Precision.HIGHEST


def blend(pattern, first_operand, second_operand):
    return jnp.einsum(pattern, first_operand, second_operand, preferred_element_type=jnp.float32)


def exact(pattern, first_operand, second_operand):
    return jnp.einsum(pattern, first_operand, second_operand, precision=EXACT)


def split_heads(row_data, head_count):
    return row_data.reshape(
        row_data.shape[0], row_data.shape[1], head_count, row_data.shape[2] // head_count
    )


def decay_tables(log_decay, restart):
    summed = jnp.cumsum(log_decay, axis=1)
    resets = jnp.cumsum(restart, axis=1, dtype=jnp.int32)
    last_total = summed[:, -1, :]
    last_reset = resets[:, -1:]
    entry_decay = jnp.where((resets == 0)[:, :, None], jnp.exp(summed), 0.0)
    exit_decay = jnp.where(
        (resets == last_reset)[:, :, None], jnp.exp(last_total[:, None, :] - summed), 0.0
    )
    block_carry = jnp.where(last_reset == 0, jnp.exp(last_total), 0.0)
    by_head = jnp.transpose(summed, (0, 2, 1))
    spread = by_head[:, :, :, None] - by_head[:, :, None, :]
    row_index = lax.broadcasted_iota(jnp.int32, spread.shape, 2)
    col_index = lax.broadcasted_iota(jnp.int32, spread.shape, 3)
    allowed = (row_index >= col_index) & (resets[:, None, :, None] == resets[:, None, None, :])
    pair_decay = jnp.exp(jnp.where(allowed, spread, -1e30))
    return (entry_decay, exit_decay, block_carry, pair_decay)


def block_state(key_heads, value_heads, exit_decay):
    decayed_keys = key_heads.astype(jnp.float32) * exit_decay[..., None]
    return (exact("bjhe,bjhf->bhef", decayed_keys, value_heads.astype(jnp.float32)), decayed_keys)


def block_forward(
    query_heads,
    key_heads,
    value_heads,
    entry_decay,
    pair_decay,
    state_in,
    norm_gain,
    upstream_heads,
):
    head_count = query_heads.shape[2]
    scores = blend("bihe,bjhe->bhij", query_heads, key_heads)
    weights = (scores * pair_decay).astype(jnp.bfloat16)
    local_part = blend("bhij,bjhe->bihe", weights, value_heads)
    decayed_queries = query_heads.astype(jnp.float32) * entry_decay[..., None]
    carried_part = exact("bihe,bhef->bihf", decayed_queries, state_in)
    mixture = local_part + carried_part
    inverse = lax.rsqrt(jnp.mean(mixture * mixture, axis=-1, keepdims=True) + EPSILON)
    normed = mixture * inverse
    gain_heads = norm_gain.reshape(head_count, -1)
    layer_out = (normed * gain_heads).astype(jnp.bfloat16)
    upstream_float = upstream_heads.astype(jnp.float32)
    gain_part = jnp.sum(upstream_float * normed, axis=(0, 1))
    grad_normed = upstream_float * gain_heads
    grad_mixed = (
        inverse * (grad_normed - normed * jnp.mean(grad_normed * normed, axis=-1, keepdims=True))
    ).astype(jnp.bfloat16)
    query_state = exact("bihe,bihf->bhef", decayed_queries, grad_mixed.astype(jnp.float32))
    flat_out = layer_out.reshape(layer_out.shape[0], layer_out.shape[1], -1)
    return (scores, weights, carried_part, flat_out, gain_part, grad_mixed, query_state)


def block_backward(
    query_heads,
    key_heads,
    value_heads,
    entry_decay,
    exit_decay,
    block_carry,
    pair_decay,
    scores,
    weights,
    carried_part,
    decayed_keys,
    grad_mixed,
    state_in,
    state_grad,
):
    grad_pairs = blend("bihe,bjhe->bhij", grad_mixed, value_heads)
    grad_weights = (grad_pairs * pair_decay).astype(jnp.bfloat16)
    mixed_float = grad_mixed.astype(jnp.float32)
    values_float = value_heads.astype(jnp.float32)
    grad_query = blend("bhij,bjhe->bihe", grad_weights, key_heads) + exact(
        "bihf,bhef->bihe", mixed_float * entry_decay[..., None], state_in
    )
    grad_key = blend("bhij,bihe->bjhe", grad_weights, query_heads) + exact(
        "bjhf,bhef->bjhe", values_float * exit_decay[..., None], state_grad
    )
    carried_value = exact("bjhe,bhef->bjhf", decayed_keys, state_grad)
    grad_value = blend("bhij,bihe->bjhe", weights, grad_mixed) + carried_value
    pair_terms = scores * grad_pairs * pair_decay
    balance = jnp.sum(pair_terms, axis=3) - jnp.sum(pair_terms, axis=2)
    later_terms = jnp.transpose(balance, (0, 2, 1)) + jnp.sum(carried_part * mixed_float, axis=-1)
    earlier_terms = jnp.sum(carried_value * values_float, axis=-1)
    through = block_carry * jnp.sum(state_in * state_grad, axis=(2, 3))
    grad_decay = (
        jnp.flip(jnp.cumsum(jnp.flip(later_terms, 1), axis=1), 1)
        + (jnp.cumsum(earlier_terms, axis=1) - earlier_terms)
        + through[:, None, :]
    )
    row_shape = (grad_query.shape[0], grad_query.shape[1], -1)
    return (
        grad_query.reshape(row_shape).astype(jnp.bfloat16),
        grad_key.reshape(row_shape).astype(jnp.bfloat16),
        grad_value.reshape(row_shape).astype(jnp.bfloat16),
        grad_decay,
    )


def weighted_sum(block_weights, fragment):
    return jnp.sum(block_weights[..., None, None] * fragment, axis=0)


def local(queries, key_vectors, value_vectors, log_decay, restart, norm_gain, upstream):
    entry_decay, exit_decay, block_carry, pair_decay = decay_tables(log_decay, restart)
    query_heads = split_heads(queries, HEAD_TOTAL)
    key_heads = split_heads(key_vectors, HEAD_TOTAL)
    value_heads = split_heads(value_vectors, HEAD_TOTAL)
    upstream_heads = split_heads(upstream, HEAD_TOTAL)
    state_part, decayed_keys = block_state(key_heads, value_heads, exit_decay)
    every_carry = lax.all_gather(block_carry[None], "seq", axis=0, tiled=True)
    position = lax.axis_index("seq")
    ranks = jnp.arange(lax.axis_size("seq"), dtype=jnp.int32)
    source = ranks[:, None]
    middle = ranks[None, :]
    factors = every_carry[None]
    before_span = (middle > source) & (middle < position)
    before_weight = jnp.where(
        (ranks < position)[:, None, None],
        jnp.prod(jnp.where(before_span[:, :, None, None], factors, 1.0), axis=1),
        0.0,
    )
    after_span = (middle > position) & (middle < source)
    after_weight = jnp.where(
        (ranks > position)[:, None, None],
        jnp.prod(jnp.where(after_span[:, :, None, None], factors, 1.0), axis=1),
        0.0,
    )
    state_in = weighted_sum(
        before_weight, lax.all_gather(state_part[None], "seq", axis=0, tiled=True)
    )
    results = block_forward(
        query_heads,
        key_heads,
        value_heads,
        entry_decay,
        pair_decay,
        state_in,
        norm_gain,
        upstream_heads,
    )
    scores, weights, carried_part, layer_out, gain_part, grad_mixed, query_state = results
    grad_gain = lax.psum(gain_part.reshape(-1), ("seq", "dp"))
    state_grad = weighted_sum(
        after_weight, lax.all_gather(query_state[None], "seq", axis=0, tiled=True)
    )
    grad_query, grad_key, grad_value, grad_decay = block_backward(
        query_heads,
        key_heads,
        value_heads,
        entry_decay,
        exit_decay,
        block_carry,
        pair_decay,
        scores,
        weights,
        carried_part,
        decayed_keys,
        grad_mixed,
        state_in,
        state_grad,
    )
    return (layer_out, grad_query, grad_key, grad_value, grad_decay, grad_gain)


def solution(mesh):
    return jax.shard_map(
        local,
        mesh=mesh,
        in_specs=(
            P("dp", "seq", None),
            P("dp", "seq", None),
            P("dp", "seq", None),
            P("dp", "seq", None),
            P("dp", "seq"),
            P(),
            P("dp", "seq", None),
        ),
        out_specs=(
            P("dp", "seq", None),
            P("dp", "seq", None),
            P("dp", "seq", None),
            P("dp", "seq", None),
            P("dp", "seq", None),
            P(),
        ),
        check_vma=False,
    )
```

profile of v0, /device:TPU:1, one launch (start us, length us, event | category | flops | bytes accessed | tf_op | source)
XLA Modules:
  0.0 276.0 jit_solution(11302597584005054084)
XLA Ops:
  7.2 1.0 reduce_window_sum.36
  8.2 0.6 slice.6
  9.5 0.7 broadcast_compare_fusion.1
  10.1 0.8 copy.78
  10.9 0.2 reduce_window_sum.37
  11.1 0.1 fusion.27
  11.3 1.1 copy.77
  12.4 1.1 copy.81
  13.5 1.4 fusion.12
  15.0 0.8 mul.158
  15.8 37.4 %all_gather.9 = f32[32,1,16]{2,1,0:T(1,128)S(1)} all-gather(f32[1,1,16]{2,1,0:T(1,128)S(1)} %get-tuple-element.40), channel_id=1, replica_groups=mesh['seq'=32,'dp'=16] {'seq'}, dimensions={0}, use_global_device_ids=true | all-gather | bytes 2112 | tf_op jit(solution)/shard_map/all_gather | solution.py:141
  53.2 1.1 copy.76
  54.4 1.1 copy.86
  55.5 1.2 select_reduce_fusion
  56.7 0.1 broadcast_compare_fusion
  56.8 0.1 broadcast_select_fusion.1
  56.9 1.4 fusion.31
  58.2 69.4 %all-gather.5.cloned.1.call-done = f32[512,64,64]{2,1,0:T(8,128)} async-done(((f32[16,64,64]{2,1,0:T(8,128)}), f32[512,64,64]{2,1,0:T(8,128)}) %all-gather.5.cloned.1.call-update) | async-done | bytes 8388624 | tf_op jit(solution)/shard_map/all_gather | solution.py:160
  127.6 7.5 %multiply_reduce_fusion.1 = f32[16,64,64]{2,1,0:T(8,128)S(1)} fusion(f32[32,1,16,64,64]{4,3,2,0,1:T(8,128)} %bitcast.105, f32[32,16]{1,0:T(8,128)S(1)} %broadcast_select_fusion.1), kind=kLoop, calls=%fused_computation.1 | loop fusion | flops 4128768 | bytes 8652800 | tf_op jit(solution)/shard_map/reduce_sum | solution.py:131
  135.1 1.0 convolution_bitcast_fusion.5
  136.1 1.8 multiply_reduce_fusion.6
  137.9 0.4 multiply_reduce_fusion.2
  138.4 0.2 multiply_convert_fusion.2
  138.6 1.3 fusion.11
  140.0 0.1 copy.90
  140.1 0.1 broadcast_select_fusion
  140.2 0.1 reshape.556
  140.2 0.9 copy.92
  141.1 0.1 fusion.8
  141.2 3.0 %fusion.23 = (f32[16,128]{1,0:T(8,128)S(1)}, f32[16,128]{1,0:T(8,128)S(1)}, f32[16,128,128]{2,1,0:T(8,128)}) fusion(f32[16,128]{1,0:T(8,128)S(1)} %copy.79, pred[128,128]{1,0:T(8,128)(4,1)S(1)} %broadcast_compare_fusion, f32[16,128,128]{2,1,0:T(8,128)} %fusion.31, bf16[128,16,64]{0,2,1:T(8,128)(2,1)S(1)} %bitcast.118, ...), kind=kOutput, calls=%fused_computation.50 | convolution fusion | flops 35647488 | bytes 2662400 | tf_op jit(solution)/shard_map/bihe,bjhe->bhij/dot_general | solution.py:14
  144.1 0.1 rev.7
  144.2 0.1 copy.89
  144.3 0.2 reduce_window_sum.39
  144.5 1.8 convolution_bitcast_fusion.2
  146.3 0.7 fusion.3
  147.0 0.8 copy.93
  147.8 105.7 %psum.7 = f32[1024]{0:T(1024)} all-reduce(f32[1024]{0:T(1024)S(1)} %reshape.556), channel_id=1, replica_groups=mesh['seq'=32,'dp'=16] {'seq','dp'}, use_global_device_ids=true, to_apply=%region_16.17 | all-reduce | flops 1024 | bytes 8192 | tf_op jit(solution)/shard_map/psum | solution.py:173
  253.5 1.8 convolution_bitcast_fusion
  255.3 7.5 %multiply_reduce_fusion = f32[16,64,64]{2,1,0:T(8,128)S(1)} fusion(f32[32,1,16,64,64]{4,3,2,0,1:T(8,128)} %bitcast.106, f32[32,16]{1,0:T(8,128)S(1)} %broadcast_select_fusion), kind=kLoop, calls=%fused_computation | loop fusion | flops 4128768 | bytes 8652800 | tf_op jit(solution)/shard_map/reduce_sum | solution.py:131
  262.8 0.2 multiply_reduce_fusion.3
  263.1 1.0 multiply_reduce_fusion.4
  264.1 0.1 copy.91
  264.2 0.2 reduce_window_sum.40
  264.3 1.8 fusion.2
  266.1 0.9 copy.95
  267.0 0.7 copy.96
  267.7 0.7 fusion.4
  268.3 0.8 copy.94
  (21 shorter events, 0.4 us)
Async XLA Ops:
  7.2 132.8 %copy-start = (bf16[1,128,1024]{2,1,0:T(8,128)(2,1)S(1)}, bf16[1,128,1024]{2,1,0:T(8,128)(2,1)}, u32[]{:S(2)}) copy-start(bf16[1,128,1024]{2,1,0:T(8,128)(2,1)} %param.9) | copy-start | bytes 786436
  7.2 120.5 %all-gather.5.cloned.1.call-start = ((), (), s32[]{:S(2)}) async-start(), calls=%async_computation | async-start | bytes 17301504 | tf_op jit(solution)/shard_map/all_gather | solution.py:160
  14.9 240.4 %all-gather.7.cloned.1.call-start = ((), (), s32[]{:S(2)}) async-start(), calls=%async_computation.1 | async-start | bytes 17301504 | tf_op jit(solution)/shard_map/all_gather | solution.py:175
Sparse Core Ops, SparseCore 0:
  15.0 112.5 all-gather.4
  140.1 107.4 all-gather.6
where the time goes:
time: 277 us; the launch traced here: 276 us
  blocking collectives  143 us (52%)
  waiting for transfers between devices  69.5 us (25%)
  other arithmetic  19.7 us (7%)
  matrix products  17.4 us (6%)
  between operations  14.9 us (5%)
  local copies, waits for them, and re-layouts  11.4 us (4%)
    psum x1, blocking collectives, local(): grad_gain = lax.psum(gain_part.reshape(-1), ('seq', 'dp'))  106 us
    all_gather x1, waiting for transfers between devices, local(): lax.all_gather(state_part[None], 'seq', axis=0, tiled=True)  69.4 us
    all_gather x1, blocking collectives, local(): every_carry = lax.all_gather(block_carry[None], 'seq', axis=0, tiled=True)  37.4 us
    reduce_sum x2, other arithmetic, weighted_sum(): return jnp.sum(block_weights[..., None, None] * fragment, axis=0)  15 us
    dot_general x6, matrix products, blend(): jnp.einsum(pattern, first_operand, second_operand, preferred_element_type...  11.4 us
    unnamed x11, local copies, waits for them, and re-layouts  8.28 us
    dot_general x6, matrix products, exact(): return jnp.einsum(pattern, first_operand, second_operand, precision=EXACT)  6.06 us
  transfers between devices with their start and end apart: 2, of which 1 were waited for; matrix products, arithmetic and copies ran while one was open for 6% of the time, Pallas kernels for 0%

commit v1 on v0

v1 whole, which is shorter than its diff:
```python
import functools

import jax
import jax.numpy as jnp
from jax import lax
from jax.experimental import pallas as pl
from jax.experimental.pallas import tpu as pltpu
from jax.sharding import PartitionSpec as P

MESH = pl.DeviceIdType.MESH
HEADS = 16
PAIRS = HEADS // 2
MINE = PAIRS // 2
TOK = 128
LANES = 128
HALF = 64
CHIPS = 16
ROWS = MINE * HALF // CHIPS
EPSILON = 1e-06
F32 = jnp.float32
BF16 = jnp.bfloat16
FAR_FIRST = (8, 7, 9, 6, 10, 5, 11, 4, 12, 3, 13, 2, 14, 1, 15)


def mm(a, b):
    return jnp.dot(a, b, preferred_element_type=F32)


def mm_t(a, b):
    return lax.dot_general(a, b, (((1,), (1,)), ((), ())), preferred_element_type=F32)


def t_mm(a, b):
    return lax.dot_general(a, b, (((0,), (0,)), ((), ())), preferred_element_type=F32)


def split_mm(a, b):
    high = a.astype(BF16)
    low = (a - high.astype(F32)).astype(BF16)
    return mm(high, b) + mm(low, b)


def split_mm_left(a, b):
    high = b.astype(BF16)
    low = (b - high.astype(F32)).astype(BF16)
    return mm(a, high) + mm(a, low)


def kernel(
    q_hbm, k_hbm, v_hbm, u_hbm, ld_ref, rs_ref, gain_ref,
    out_ref, dq_ref, dk_ref, dv_ref, dd_ref, dg_ref,
    q_s, k_s, v_s, u_s, in_sem,
    entry_s, exit_s, p_s, pt_s, sp_s, spt_s, loc_s, car_s, qet_s, g_s, dkl_s, dvl_s,
    st_own, st_oth, qs_own, qs_oth, carr_own, carr_oth, si_s, si_x, sg_s, sg_x,
    send1, recv1, send2, recv2, send3, recv3, send4, recv4,
    gain_own, gain_oth, gain_z, gain_all,
    x_send, x_recv, p_send, p_recv, g_send, g_recv,
):
    seq = lax.axis_index("seq")
    dp = lax.axis_index("dp")
    z = seq // 2
    core = lax.rem(seq, 2)
    partner = z * 2 + (1 - core)

    def chip(index):
        return index * 2 + core

    barrier = pltpu.get_barrier_semaphore()
    for step in FAR_FIRST:
        pl.semaphore_signal(barrier, inc=1, device_id={"seq": chip(lax.rem(z + step, CHIPS))}, device_id_type=MESH)
    for step in range(1, 16):
        pl.semaphore_signal(barrier, inc=1, device_id={"dp": lax.rem(dp + step, 16)}, device_id_type=MESH)
    pl.semaphore_signal(barrier, inc=1, device_id={"seq": partner}, device_id_type=MESH)

    loads = [
        pltpu.make_async_copy(source, target, in_sem.at[i])
        for i, (source, target) in enumerate(((k_hbm, k_s), (v_hbm, v_s), (q_hbm, q_s), (u_hbm, u_s)))
    ]
    for load in loads:
        load.start()

    def lanes(pair):
        return slice(pair * LANES, (pair + 1) * LANES)

    row_i = lax.broadcasted_iota(jnp.int32, (TOK, TOK), 0)
    col_i = lax.broadcasted_iota(jnp.int32, (TOK, TOK), 1)
    low = col_i < HALF
    low_half = low[:HALF]
    tri = row_i >= col_i

    def both(column_a, column_b):
        return jnp.where(low, column_a, column_b)

    def stack(x):
        zero = jnp.zeros_like(x)
        return jnp.concatenate([jnp.where(low, x, zero), jnp.where(low, zero, x)], axis=0)

    def compact(x):
        return jnp.where(low_half, x[:HALF], x[HALF:])

    def block_diagonal(x):
        zero = jnp.zeros_like(x)
        return jnp.concatenate([jnp.where(low_half, x, zero), jnp.where(low_half, zero, x)], axis=0)

    marks = rs_ref[...].astype(F32)
    resets_col = jnp.sum(jnp.where(tri, marks, 0.0), axis=1, keepdims=True)
    resets_row = mm(jnp.broadcast_to(marks, (8, TOK)).astype(BF16), (row_i <= col_i).astype(BF16))[0:1]
    last_reset = resets_row[:, TOK - 1 :]
    cum = jnp.dot(tri.astype(F32), ld_ref[...], precision=lax.Precision.HIGHEST, preferred_element_type=F32)
    last_total = cum[TOK - 1 :, :]
    exit_all = jnp.where(resets_col == last_reset, jnp.exp(last_total - cum), 0.0)
    carry_all = jnp.where(last_reset == 0.0, jnp.exp(last_total), 0.0)
    for pair in range(PAIRS):
        a, b = 2 * pair, 2 * pair + 1
        exit_s[pair] = both(exit_all[:, a : a + 1], exit_all[:, b : b + 1])
        carr_own[pair : pair + 1, :] = jnp.where(low[0:1], carry_all[:, a : a + 1], carry_all[:, b : b + 1])

    loads[0].wait()
    loads[1].wait()
    for pair in range(PAIRS):
        decayed = (k_s[:, lanes(pair)].astype(F32) * exit_s[pair]).astype(BF16)
        st_own[pair] = compact(t_mm(decayed, v_s[:, lanes(pair)]))

    pl.semaphore_wait(barrier, 31)

    theirs = pl.ds(MINE * (1 - core), MINE)
    mine = pl.ds(MINE * core, MINE)

    def to_partner(source, target, index):
        return pltpu.make_async_remote_copy(
            source, target, x_send.at[index], x_recv.at[index], device_id={"seq": partner}, device_id_type=MESH
        )

    def to_chip(phase, source, target, there):
        return pltpu.make_async_remote_copy(
            source, target.at[z], p_send.at[phase, there], p_recv.at[phase, z],
            device_id={"seq": chip(there)}, device_id_type=MESH,
        )

    def from_chip(phase, source, target, there):
        return pltpu.make_async_remote_copy(
            source, target.at[there], p_send.at[phase, there], p_recv.at[phase, there],
            device_id={"seq": chip(there)}, device_id_type=MESH,
        )

    carry_swap = to_partner(carr_own, carr_oth, 0)
    state_swap = to_partner(st_own.at[theirs], st_oth, 1)
    carry_swap.start()
    state_swap.start()
    carry_swap.wait_recv()
    state_swap.wait_recv()

    first = core == 0

    def in_order(own, other):
        return jnp.where(first, own, other), jnp.where(first, other, own)

    carry_0, carry_1 = in_order(carr_own[...], carr_oth[...])
    for pair in range(MINE):
        index = MINE * core + pair
        s_0, s_1 = in_order(st_own[index], st_oth[pair])
        c_0, c_1 = in_order(carr_own[pl.ds(index, 1), :], carr_oth[pl.ds(index, 1), :])
        send1[pair * 4 : pair * 4 + 4, :ROWS, :] = (c_1 * s_0 + s_1).reshape(4, ROWS, LANES)
        send1[pair * 4 : pair * 4 + 4, ROWS:, :] = jnp.broadcast_to(c_0 * c_1, (4, 8, LANES))
    for step in FAR_FIRST:
        there = lax.rem(z + step, CHIPS)
        to_chip(0, send1.at[there], recv1, there).start()
    recv1[z] = send1[z]

    entry_all = jnp.where(resets_col == 0.0, jnp.exp(cum), 0.0)
    same = resets_col == resets_row
    allowed = tri & same
    allowed_t = (row_i <= col_i) & same
    cum_t = cum.T
    for head in range(HEADS):
        column, row = cum[:, head : head + 1], cum_t[head : head + 1, :]
        spread = column - row
        rows = slice((head % 2) * TOK, (head % 2 + 1) * TOK)
        p_s[head // 2, rows] = jnp.exp(jnp.where(allowed, spread, -1e30))
        pt_s[head // 2, rows] = jnp.exp(jnp.where(allowed_t, -spread, -1e30))
    for pair in range(PAIRS):
        a, b = 2 * pair, 2 * pair + 1
        entry_s[pair] = both(entry_all[:, a : a + 1], entry_all[:, b : b + 1])
    loads[2].wait()
    loads[3].wait()
    for pair in range(PAIRS):
        q, k, v = q_s[:, lanes(pair)], k_s[:, lanes(pair)], v_s[:, lanes(pair)]
        sp = mm_t(stack(q), k) * p_s[pair]
        sp_s[pair] = sp
        weights = sp.astype(BF16)
        v_2 = stack(v)
        loc_s[pair] = mm(weights[:TOK], v_2[:TOK]) + mm(weights[TOK:], v_2[TOK:])

    state = jnp.zeros((ROWS, LANES), F32)
    for there in range(CHIPS):

        @pl.when(z != there)
        def _():
            from_chip(0, send1.at[there], recv1, there).wait_recv()

        send2[there] = state

        @pl.when(z != there)
        def _():
            to_chip(1, send2.at[there], recv2, there).start()

        state = recv1[there, ROWS : ROWS + 1, :] * state + recv1[there, :ROWS, :]
    recv2[z] = send2[z]

    for pair in range(PAIRS):
        q, k = q_s[:, lanes(pair)], k_s[:, lanes(pair)]
        spt_s[pair] = mm_t(stack(k), q) * pt_s[pair]
        qet_s[pair] = (q.astype(F32) * entry_s[pair]).T.astype(BF16)

    for step in range(1, CHIPS):
        there = lax.rem(z + step, CHIPS)
        from_chip(1, send2.at[there], recv2, there).wait_recv()
    for pair in range(MINE):
        index = MINE * core + pair
        s_0, _ = in_order(st_own[index], st_oth[pair])
        c_0, _ = in_order(carr_own[pl.ds(index, 1), :], carr_oth[pl.ds(index, 1), :])
        arrived = recv2[pair * 4 : pair * 4 + 4].reshape(HALF, LANES)
        own, other = in_order(arrived, c_0 * arrived + s_0)
        si_s[index] = own
        si_x[pair] = other
    in_swap = to_partner(si_x, si_s.at[mine], 2)
    in_swap.start()
    in_swap.wait_recv()

    mean_of = jnp.where((row_i < HALF) == low, 1.0 / HALF, 0.0).astype(BF16)
    for pair in range(PAIRS):
        q = q_s[:, lanes(pair)]
        gain = gain_ref[:, lanes(pair)]
        carried = entry_s[pair] * mm(q, block_diagonal(si_s[pair]).astype(BF16))
        car_s[pair] = carried
        mixture = loc_s[pair] + carried
        inverse = lax.rsqrt(split_mm(mixture * mixture, mean_of) + EPSILON)
        normed = mixture * inverse
        out_ref[:, lanes(pair)] = (normed * gain).astype(BF16)
        up = u_s[:, lanes(pair)].astype(F32)
        gain_own[pair : pair + 1, :] = jnp.sum(up * normed, axis=0, keepdims=True)
        grad = up * gain
        shift = split_mm(grad * normed, mean_of)
        mixed = (inverse * (grad - normed * shift)).astype(BF16)
        g_s[pair] = mixed
        qs_own[pair] = compact(mm(qet_s[pair], mixed))

    query_swap = to_partner(qs_own.at[theirs], qs_oth, 3)
    gain_swap = to_partner(gain_own, gain_oth, 4)
    query_swap.start()
    gain_swap.start()
    query_swap.wait_recv()
    gain_swap.wait_recv()
    gain_chip = gain_own[...] + gain_oth[...]
    for pair in range(MINE):
        index = MINE * core + pair
        s_0, s_1 = in_order(qs_own[index], qs_oth[pair])
        c_0, _ = in_order(carr_own[pl.ds(index, 1), :], carr_oth[pl.ds(index, 1), :])
        send3[pair * 4 : pair * 4 + 4, :ROWS, :] = (s_0 + c_0 * s_1).reshape(4, ROWS, LANES)
        send3[pair * 4 : pair * 4 + 4, ROWS:, :] = jnp.broadcast_to(gain_chip[None], (4, 8, LANES))
    for step in FAR_FIRST:
        there = lax.rem(z + step, CHIPS)
        to_chip(2, send3.at[there], recv3, there).start()
    recv3[z] = send3[z]

    head_i = lax.broadcasted_iota(jnp.int32, (LANES, HEADS), 1)
    half_i = (lax.broadcasted_iota(jnp.int32, (LANES, HEADS), 0) >= HALF).astype(jnp.int32)
    column_i = lax.broadcasted_iota(jnp.int32, (TOK, HEADS), 1)

    def head_of(pair):
        return (head_i == 2 * pair + half_i).astype(BF16)

    later = jnp.zeros((TOK, HEADS), F32)
    for pair in range(PAIRS):
        q, k, v = q_s[:, lanes(pair)], k_s[:, lanes(pair)], v_s[:, lanes(pair)]
        mixed = g_s[pair]
        pairs = mm_t(stack(mixed), v)
        grad_weights = (pairs * p_s[pair]).astype(BF16)
        k_2 = stack(k)
        query_state = block_diagonal(si_s[pair]).astype(BF16)
        dq = mm(grad_weights[:TOK], k_2[:TOK]) + mm(grad_weights[TOK:], k_2[TOK:]) + entry_s[pair] * mm_t(mixed, query_state)
        dq_ref[:, lanes(pair)] = dq.astype(BF16)
        pairs_t = mm_t(stack(v), mixed)
        grad_weights_t = (pairs_t * pt_s[pair]).astype(BF16)
        q_2 = stack(q)
        dkl_s[pair] = mm(grad_weights_t[:TOK], q_2[:TOK]) + mm(grad_weights_t[TOK:], q_2[TOK:])
        weights_t = spt_s[pair].astype(BF16)
        g_2 = stack(mixed)
        dvl_s[pair] = mm(weights_t[:TOK], g_2[:TOK]) + mm(weights_t[TOK:], g_2[TOK:])
        balance = jnp.sum(sp_s[pair] * pairs - spt_s[pair] * pairs_t, axis=1, keepdims=True)
        later = later + jnp.where(column_i == 2 * pair, balance[:TOK], 0.0)
        later = later + jnp.where(column_i == 2 * pair + 1, balance[TOK:], 0.0)
        later = later + split_mm(car_s[pair] * mixed.astype(F32), head_of(pair))

    state = jnp.zeros((ROWS, LANES), F32)
    gain_sum = jnp.zeros((8, LANES), F32)
    for there in reversed(range(CHIPS)):

        @pl.when(z != there)
        def _():
            from_chip(2, send3.at[there], recv3, there).wait_recv()

        send4[there] = state

        @pl.when(z != there)
        def _():
            to_chip(3, send4.at[there], recv4, there).start()

        state = recv1[there, ROWS : ROWS + 1, :] * state + recv3[there, :ROWS, :]
        gain_sum = gain_sum + recv3[there, ROWS:, :]
    recv4[z] = send4[z]
    gain_z[...] = gain_sum
    gain_all[dp] = gain_sum

    def to_scan(there):
        return pltpu.make_async_remote_copy(
            gain_z, gain_all.at[dp], g_send.at[there], g_recv.at[dp], device_id={"dp": there}, device_id_type=MESH
        )

    def from_scan(there):
        return pltpu.make_async_remote_copy(
            gain_z, gain_all.at[there], g_send.at[there], g_recv.at[there], device_id={"dp": there}, device_id_type=MESH
        )

    for step in range(1, 16):
        to_scan(lax.rem(dp + step, 16)).start()

    later_sum = split_mm_left((row_i <= col_i).astype(BF16), later)

    for step in range(1, CHIPS):
        there = lax.rem(z + step, CHIPS)
        from_chip(3, send4.at[there], recv4, there).wait_recv()
    for pair in range(MINE):
        index = MINE * core + pair
        _, s_1 = in_order(qs_own[index], qs_oth[pair])
        _, c_1 = in_order(carr_own[pl.ds(index, 1), :], carr_oth[pl.ds(index, 1), :])
        arrived = recv4[pair * 4 : pair * 4 + 4].reshape(HALF, LANES)
        own, other = in_order(s_1 + c_1 * arrived, arrived)
        sg_s[index] = own
        sg_x[pair] = other
    grad_swap = to_partner(sg_x, sg_s.at[mine], 5)
    grad_swap.start()
    grad_swap.wait_recv()

    earlier = jnp.zeros((TOK + 8, HEADS), F32)
    for pair in range(PAIRS):
        k, v = k_s[:, lanes(pair)], v_s[:, lanes(pair)]
        state_grad = block_diagonal(sg_s[pair]).astype(BF16)
        dk_ref[:, lanes(pair)] = (dkl_s[pair] + exit_s[pair] * mm_t(v, state_grad)).astype(BF16)
        carried_value = exit_s[pair] * mm(k, state_grad)
        dv_ref[:, lanes(pair)] = (dvl_s[pair] + carried_value).astype(BF16)
        through = jnp.sum(si_s[pair] * sg_s[pair], axis=0, keepdims=True) * carr_own[pair : pair + 1, :]
        terms = jnp.concatenate([carried_value * v.astype(F32), jnp.broadcast_to(through, (8, LANES))], axis=0)
        earlier = earlier + split_mm(terms, head_of(pair))
    dd_ref[...] = later_sum + split_mm_left((row_i > col_i).astype(BF16), earlier[:TOK]) + earlier[TOK : TOK + 1]

    for step in range(1, 16):
        from_scan(lax.rem(dp + step, 16)).wait_recv()
    dg_ref[...] = jnp.sum(gain_all[...], axis=0)

    for swap in (carry_swap, state_swap, in_swap, query_swap, gain_swap, grad_swap):
        swap.wait_send()
    for step in range(1, CHIPS):
        there = lax.rem(z + step, CHIPS)
        for phase, (source, target) in enumerate(((send1, recv1), (send2, recv2), (send3, recv3), (send4, recv4))):
            to_chip(phase, source.at[there], target, there).wait_send()
    for step in range(1, 16):
        to_scan(lax.rem(dp + step, 16)).wait_send()


def local(queries, key_vectors, value_vectors, log_decay, restart, norm_gain, upstream):
    width = queries.shape[-1]
    vmem = pl.BlockSpec(memory_space=pltpu.VMEM)
    hbm = pl.BlockSpec(memory_space=pl.ANY)
    wide = pltpu.VMEM((TOK, width), BF16)
    table = pltpu.VMEM((PAIRS, TOK, LANES), F32)
    table_bf16 = pltpu.VMEM((PAIRS, TOK, LANES), BF16)
    double = pltpu.VMEM((PAIRS, 2 * TOK, LANES), F32)
    states = pltpu.VMEM((PAIRS, HALF, LANES), F32)
    some_states = pltpu.VMEM((MINE, HALF, LANES), F32)
    tile = pltpu.VMEM((8, LANES), F32)
    slices = pltpu.VMEM((CHIPS, ROWS, LANES), F32)
    slices_and = pltpu.VMEM((CHIPS, ROWS + 8, LANES), F32)
    dma = pltpu.SemaphoreType.DMA
    rows = jax.ShapeDtypeStruct((TOK, width), BF16)
    outs = pl.pallas_call(
        kernel,
        out_shape=(
            rows, rows, rows, rows,
            jax.ShapeDtypeStruct((TOK, HEADS), F32),
            jax.ShapeDtypeStruct((8, LANES), F32),
        ),
        in_specs=[hbm] * 4 + [vmem] * 3,
        out_specs=[vmem] * 6,
        scratch_shapes=[
            wide, wide, wide, wide, dma((4,)),
            table, table, double, double, double, double, table, table, table_bf16, table_bf16, table, table,
            states, some_states, states, some_states, tile, tile, states, some_states, states, some_states,
            slices_and, slices_and, slices, slices, slices_and, slices_and, slices, slices,
            tile, tile, tile, pltpu.VMEM((16, 8, LANES), F32),
            dma((6,)), dma((6,)), dma((4, CHIPS)), dma((4, CHIPS)), dma((16,)), dma((16,)),
        ],
        compiler_params=pltpu.CompilerParams(collective_id=0, has_side_effects=True, vmem_limit_bytes=48 * 1024 * 1024),
    )(
        queries[0], key_vectors[0], value_vectors[0], upstream[0], log_decay[0], restart, norm_gain.reshape(1, width)
    )
    layer_out, dq, dk, dv, dd, dg = outs
    return (layer_out[None], dq[None], dk[None], dv[None], dd[None], dg.reshape(-1))


def solution(mesh):
    row, narrow = P("dp", "seq", None), P("dp", "seq")
    return jax.shard_map(
        local,
        mesh=mesh,
        in_specs=(row, row, row, row, narrow, P(), row),
        out_specs=(row, row, row, row, row, P()),
        check_vma=False,
    )
```

time: 277 us -> 77.2 us (0.28)
  blocking collectives: 143 us -> 0 us
  waiting for transfers between devices: 69.5 us -> 0 us
  Pallas kernels: 0 us -> 66.2 us
  other arithmetic: 19.7 us -> 0 us
  matrix products: 17.4 us -> 0 us
  between operations: 14.9 us -> 0.66 us
    psum x1 -> x0, blocking collectives: 106 us -> none  [local(): grad_gain = lax.psum(gain_part.reshape(-1), ('seq', 'dp'))]
    all_gather x2 -> x0, waiting for transfers between devices: 69.4 us -> none  [the longest x1 69.4 us: local(): lax.all_gather(state_part[None], 'seq', axis=0, tiled=True)]
    pallas_call x0 -> x1, Pallas kernels: none -> 66.2 us  [local(): pl.pallas_call(kernel, out_shape=(rows, rows, rows, rows, jax.ShapeDtypeS...]
    all_gather x1 -> x0, blocking collectives: 37.4 us -> none  [local(): every_carry = lax.all_gather(block_carry[None], 'seq', axis=0, tiled=True)]
    dot_general x12 -> x0, matrix products: 17.4 us -> none  [the longest x6 11.4 us: blend(): jnp.einsum(pattern, first_operand, second_operand, preferred_element_type...]
    reduce_sum x5 -> x0, other arithmetic: 15.7 us -> none  [the longest x2 15 us: weighted_sum(): return jnp.sum(block_weights[..., None, None] * fragment, axis=0)]
    unnamed x11 -> x21, local copies, waits for them, and re-layouts: 8.28 us -> 9.31 us
  transfers between devices with their start and end apart: 2 -> 0, of which waited for: 1 -> 0; matrix products, arithmetic and copies ran while one was open for 6% -> 0% of each run, Pallas kernels for 0% -> 0%
where the time goes in v1:
time: 77.2 us; the launch traced here: 76.2 us
  Pallas kernels  66.2 us (86%)
  local copies, waits for them, and re-layouts  9.31 us (12%)
    pallas_call x1, Pallas kernels, local(): pl.pallas_call(kernel, out_shape=(rows, rows, rows, rows, jax.ShapeDtypeS...  66.2 us
    unnamed x21, local copies, waits for them, and re-layouts  9.31 us

profile of v1, /device:TPU:1, one launch (start us, length us, event | category | flops | bytes accessed | tf_op | source)
XLA Modules:
  0.0 76.2 jit_solution(14026084842936996795)
XLA Ops:
  0.6 0.0 copy-start.6
  0.6 0.7 copy-done.6
  1.3 0.0 copy-start.4
  1.3 0.1 copy.13
  1.4 0.0 copy-start.5
  1.4 0.6 copy-done.4
  2.0 0.1 copy-done.5
  2.1 0.0 copy-start
  2.1 0.9 %copy-done = bf16[1,128,1024]{2,1,0:T(8,128)(2,1)S(1)} copy-done((bf16[1,128,1024]{2,1,0:T(8,128)(2,1)S(1)}, bf16[1,128,1024]{2,1,0:T(8,128)(2,1)}, u32[]{:S(2)}) %copy-start) | copy-done | bytes 262168
  3.0 0.0 copy-start.1
  3.0 0.9 %copy-done.1 = bf16[1,128,1024]{2,1,0:T(8,128)(2,1)S(1)} copy-done((bf16[1,128,1024]{2,1,0:T(8,128)(2,1)S(1)}, bf16[1,128,1024]{2,1,0:T(8,128)(2,1)}, u32[]{:S(2)}) %copy-start.1) | copy-done | bytes 262168
  4.0 0.0 copy-start.2
  4.0 0.9 %copy-done.2 = bf16[1,128,1024]{2,1,0:T(8,128)(2,1)S(1)} copy-done((bf16[1,128,1024]{2,1,0:T(8,128)(2,1)S(1)}, bf16[1,128,1024]{2,1,0:T(8,128)(2,1)}, u32[]{:S(2)}) %copy-start.2) | copy-done | bytes 262168
  4.9 0.0 copy-start.3
  4.9 0.9 %copy-done.3 = bf16[1,128,1024]{2,1,0:T(8,128)(2,1)S(1)} copy-done((bf16[1,128,1024]{2,1,0:T(8,128)(2,1)S(1)}, bf16[1,128,1024]{2,1,0:T(8,128)(2,1)}, u32[]{:S(2)}) %copy-start.3) | copy-done | bytes 262168
  5.9 66.2 %shard_map.118 = (bf16[128,1024]{1,0:T(8,128)(2,1)S(1)}, bf16[128,1024]{1,0:T(8,128)(2,1)S(1)}, bf16[128,1024]{1,0:T(8,128)(2,1)S(1)}, bf16[128,1024]{1,0:T(8,12...) custom-call(bf16[128,1024]{1,0:T(8,128)(2,1)S(1)} %bitcast.17, bf16[128,1024]{1,0:T(8,128)(2,1)S(1)} %bitcast.18, ...), custom_call_target="tpu_custom_call" | custom-call | tf_op jit(solution)/shard_map/pallas_call | solution.py:386
  72.1 0.7 copy.14
  72.8 0.7 copy.20
  73.5 0.7 copy.21
  74.2 0.7 copy.22
  74.9 0.7 copy.23
  75.6 0.6 copy.24
Async XLA Ops:
  0.6 0.7 copy-start.6
  1.3 0.7 copy-start.4
  1.4 0.7 copy-start.5
  2.1 0.9 %copy-start = (bf16[1,128,1024]{2,1,0:T(8,128)(2,1)S(1)}, bf16[1,128,1024]{2,1,0:T(8,128)(2,1)}, u32[]{:S(2)}) copy-start(bf16[1,128,1024]{2,1,0:T(8,128)(2,1)} %param.7) | copy-start | bytes 786436
  3.0 0.9 %copy-start.1 = (bf16[1,128,1024]{2,1,0:T(8,128)(2,1)S(1)}, bf16[1,128,1024]{2,1,0:T(8,128)(2,1)}, u32[]{:S(2)}) copy-start(bf16[1,128,1024]{2,1,0:T(8,128)(2,1)} %param.8) | copy-start | bytes 786436
  4.0 0.9 %copy-start.2 = (bf16[1,128,1024]{2,1,0:T(8,128)(2,1)S(1)}, bf16[1,128,1024]{2,1,0:T(8,128)(2,1)}, u32[]{:S(2)}) copy-start(bf16[1,128,1024]{2,1,0:T(8,128)(2,1)} %param.9) | copy-start | bytes 786436
  4.9 0.9 %copy-start.3 = (bf16[1,128,1024]{2,1,0:T(8,128)(2,1)S(1)}, bf16[1,128,1024]{2,1,0:T(8,128)(2,1)}, u32[]{:S(2)}) copy-start(bf16[1,128,1024]{2,1,0:T(8,128)(2,1)} %param.13) | copy-start | bytes 786436

commit v2 on v1

v2 whole, which is shorter than its diff:
```python
import functools

import jax
import jax.numpy as jnp
from jax import lax
from jax.experimental import pallas as pl
from jax.experimental.pallas import tpu as pltpu
from jax.sharding import PartitionSpec as P

MESH = pl.DeviceIdType.MESH
HEADS = 16
PAIRS = HEADS // 2
MINE = PAIRS // 2
TOK = 128
LANES = 128
HALF = 64
CHIPS = 16
ROWS = MINE * HALF // CHIPS
SENT = ROWS + 1
EPSILON = 1e-06
F32 = jnp.float32
BF16 = jnp.bfloat16
FAR_FIRST = (8, 7, 9, 6, 10, 5, 11, 4, 12, 3, 13, 2, 14, 1, 15)


def mm(a, b):
    return jnp.dot(a, b, preferred_element_type=F32)


def mm_t(a, b):
    return lax.dot_general(a, b, (((1,), (1,)), ((), ())), preferred_element_type=F32)


def t_mm(a, b):
    return lax.dot_general(a, b, (((0,), (0,)), ((), ())), preferred_element_type=F32)


def split_mm(a, b):
    high = a.astype(BF16)
    low = (a - high.astype(F32)).astype(BF16)
    return mm(high, b) + mm(low, b)


def split_mm_left(a, b):
    high = b.astype(BF16)
    low = (b - high.astype(F32)).astype(BF16)
    return mm(a, high) + mm(a, low)


def row_peer(dp, step):
    return dp // 4 * 4 + lax.rem(dp + step, 4)


def column_peer(dp, step):
    return lax.rem(dp + 4 * step, 16)


def kernel(
    q_hbm, k_hbm, v_hbm, u_hbm, ld_hbm, rs_hbm, gain_hbm,
    out_ref, dq_ref, dk_ref, dv_ref, dd_ref, dg_ref,
    q_s, k_s, v_s, u_s, ld_ref, rs_ref, gain_ref, in_sem,
    entry_s, exit_s, p_s, pt_s, sp_s, spt_s, loc_s, car_s, qet_s, g_s, dkl_s, dvl_s,
    st_own, st_oth, qs_own, qs_oth, carr_own, carr_oth, si_s, si_x, sg_s, sg_x,
    send1, recv1, send2, recv2, send3, recv3, send4, recv4,
    gain_own, gain_oth, gain_out, gain_in,
    x_send, x_recv, p_send, p_recv, g_send, g_recv,
):
    seq = lax.axis_index("seq")
    dp = lax.axis_index("dp")
    z = seq // 2
    core = lax.rem(seq, 2)
    partner = z * 2 + (1 - core)

    def chip(index):
        return index * 2 + core

    barrier = pltpu.get_barrier_semaphore()
    for step in FAR_FIRST:
        pl.semaphore_signal(barrier, inc=1, device_id={"seq": chip(lax.rem(z + step, CHIPS))}, device_id_type=MESH)
    for step in range(1, 4):
        for there in (row_peer(dp, step), column_peer(dp, step)):
            pl.semaphore_signal(barrier, inc=1, device_id={"dp": there}, device_id_type=MESH)
    pl.semaphore_signal(barrier, inc=1, device_id={"seq": partner}, device_id_type=MESH)

    loads = [
        pltpu.make_async_copy(source, target, in_sem.at[i])
        for i, (source, target) in enumerate(
            ((ld_hbm, ld_ref), (rs_hbm, rs_ref), (k_hbm, k_s), (v_hbm, v_s), (q_hbm, q_s), (u_hbm, u_s), (gain_hbm, gain_ref))
        )
    ]
    for load in loads:
        load.start()

    def lanes(pair):
        if isinstance(pair, int):
            return slice(pair * LANES, (pair + 1) * LANES)
        return pl.ds(pl.multiple_of(pair * LANES, LANES), LANES)

    row_i = lax.broadcasted_iota(jnp.int32, (TOK, TOK), 0)
    col_i = lax.broadcasted_iota(jnp.int32, (TOK, TOK), 1)
    low = col_i < HALF
    low_half = low[:HALF]
    tri = row_i >= col_i

    def both(column_a, column_b):
        return jnp.where(low, column_a, column_b)

    def stack(x):
        zero = jnp.zeros_like(x)
        return jnp.concatenate([jnp.where(low, x, zero), jnp.where(low, zero, x)], axis=0)

    def compact(x):
        return jnp.where(low_half, x[:HALF], x[HALF:])

    def block_diagonal(x):
        zero = jnp.zeros_like(x)
        return jnp.concatenate([jnp.where(low_half, x, zero), jnp.where(low_half, zero, x)], axis=0)

    loads[0].wait()
    loads[1].wait()
    marks = rs_ref[...].astype(F32)
    resets_col = jnp.sum(jnp.where(tri, marks, 0.0), axis=1, keepdims=True)
    resets_row = mm(jnp.broadcast_to(marks, (8, TOK)).astype(BF16), (row_i <= col_i).astype(BF16))[0:1]
    last_reset = resets_row[:, TOK - 1 :]
    cum_t = jnp.dot(
        ld_ref[...], (row_i <= col_i).astype(F32), precision=lax.Precision.HIGHEST, preferred_element_type=F32
    )
    cum = cum_t.T
    last_total = cum[TOK - 1 :, :]
    exit_all = jnp.where(resets_col == last_reset, jnp.exp(last_total - cum), 0.0)
    carry_all = jnp.where(last_reset == 0.0, jnp.exp(last_total), 0.0)
    for pair in range(PAIRS):
        a, b = 2 * pair, 2 * pair + 1
        exit_s[pair] = both(exit_all[:, a : a + 1], exit_all[:, b : b + 1])
        carr_own[pair : pair + 1, :] = jnp.where(low[0:1], carry_all[:, a : a + 1], carry_all[:, b : b + 1])

    loads[2].wait()
    loads[3].wait()
    for pair in range(PAIRS):
        decayed = (k_s[:, lanes(pair)].astype(F32) * exit_s[pair]).astype(BF16)
        st_own[pair] = compact(t_mm(decayed, v_s[:, lanes(pair)]))

    pl.semaphore_wait(barrier, 22)

    group = z // 4
    far_pairs = [lax.rem(group + step, 4) for step in (2, 1, 3, 0)]
    near_pairs = far_pairs[::-1]

    def to_partner(source, target, index):
        return pltpu.make_async_remote_copy(
            source, target, x_send.at[index], x_recv.at[index], device_id={"seq": partner}, device_id_type=MESH
        )

    def to_chip(phase, source, target, there):
        return pltpu.make_async_remote_copy(
            source, target.at[z], p_send.at[phase, there], p_recv.at[phase, z],
            device_id={"seq": chip(there)}, device_id_type=MESH,
        )

    def from_chip(phase, source, target, there):
        return pltpu.make_async_remote_copy(
            source, target.at[there], p_send.at[phase, there], p_recv.at[phase, there],
            device_id={"seq": chip(there)}, device_id_type=MESH,
        )

    first = core == 0

    def in_order(own, other):
        return jnp.where(first, own, other), jnp.where(first, other, own)

    carry_swap = to_partner(carr_own, carr_oth, 0)
    state_swaps = [to_partner(st_own.at[MINE * (1 - core) + pair], st_oth.at[pair], 1 + i) for i, pair in enumerate(far_pairs)]
    carry_swap.start()
    for swap in state_swaps:
        swap.start()
    carry_swap.wait_recv()

    def carries(pair):
        index = pl.ds(MINE * core + pair, 1)
        return in_order(carr_own[index, :], carr_oth[index, :])

    def start_slices(phase, pair, source, target):
        for i in range(4):
            there = pair * 4 + i

            @pl.when(there != z)
            def _():
                to_chip(phase, source.at[there], target, there).start()

    for pair, swap in zip(far_pairs, state_swaps):
        swap.wait_recv()
        s_0, s_1 = in_order(st_own[MINE * core + pair], st_oth[pair])
        c_0, c_1 = carries(pair)
        send1[pl.ds(pair * 4, 4), :ROWS, :] = (c_1 * s_0 + s_1).reshape(4, ROWS, LANES)
        send1[pl.ds(pair * 4, 4), ROWS:, :] = jnp.broadcast_to(c_0 * c_1, (4, 8, LANES))
        start_slices(0, pair, send1.at[:, pl.ds(0, SENT)], recv1.at[:, pl.ds(0, SENT)])
    recv1[z] = send1[z]

    entry_all = jnp.where(resets_col == 0.0, jnp.exp(cum), 0.0)
    same = resets_col == resets_row
    allowed = tri & same
    allowed_t = (row_i <= col_i) & same
    for head in range(HEADS):
        column, row = cum[:, head : head + 1], cum_t[head : head + 1, :]
        spread = column - row
        rows = slice((head % 2) * TOK, (head % 2 + 1) * TOK)
        p_s[head // 2, rows] = jnp.exp(jnp.where(allowed, spread, -1e30))
        pt_s[head // 2, rows] = jnp.exp(jnp.where(allowed_t, -spread, -1e30))
    for pair in range(PAIRS):
        a, b = 2 * pair, 2 * pair + 1
        entry_s[pair] = both(entry_all[:, a : a + 1], entry_all[:, b : b + 1])
    loads[4].wait()
    loads[5].wait()
    loads[6].wait()
    for pair in range(PAIRS):
        q, k, v = q_s[:, lanes(pair)], k_s[:, lanes(pair)], v_s[:, lanes(pair)]
        sp = mm_t(stack(q), k) * p_s[pair]
        sp_s[pair] = sp
        weights = sp.astype(BF16)
        v_2 = stack(v)
        loc_s[pair] = mm(weights[:TOK], v_2[:TOK]) + mm(weights[TOK:], v_2[TOK:])

    state = jnp.zeros((ROWS, LANES), F32)
    for there in range(CHIPS):

        @pl.when(z != there)
        def _():
            from_chip(0, send1.at[there, pl.ds(0, SENT)], recv1.at[:, pl.ds(0, SENT)], there).wait_recv()

        send2[there] = state

        @pl.when(z != there)
        def _():
            to_chip(1, send2.at[there], recv2, there).start()

        state = recv1[there, ROWS : ROWS + 1, :] * state + recv1[there, :ROWS, :]
    recv2[z] = send2[z]

    for pair in range(PAIRS):
        q, k = q_s[:, lanes(pair)], k_s[:, lanes(pair)]
        spt_s[pair] = mm_t(stack(k), q) * pt_s[pair]
        qet_s[pair] = (q.astype(F32) * entry_s[pair]).T.astype(BF16)

    def wait_slices(phase, pair, source, target):
        for i in range(4):
            there = pair * 4 + i

            @pl.when(there != z)
            def _():
                from_chip(phase, source.at[there], target, there).wait_recv()

    in_swaps = []
    for i, pair in enumerate(near_pairs):
        wait_slices(1, pair, send2, recv2)
        index = MINE * core + pair
        s_0, _ = in_order(st_own[index], st_oth[pair])
        c_0, _ = carries(pair)
        arrived = recv2[pl.ds(pair * 4, 4)].reshape(HALF, LANES)
        own, other = in_order(arrived, c_0 * arrived + s_0)
        si_s[index] = own
        si_x[pair] = other
        in_swaps.append(to_partner(si_x.at[pair], si_s.at[index], 5 + i))
        in_swaps[-1].start()

    mean_of = jnp.where((row_i < HALF) == low, 1.0 / HALF, 0.0).astype(BF16)
    def mix(pair):
        q = q_s[:, lanes(pair)]
        gain = gain_ref[pl.ds(pair, 1), :]
        carried = entry_s[pair] * mm(q, block_diagonal(si_s[pair]).astype(BF16))
        car_s[pair] = carried
        mixture = loc_s[pair] + carried
        inverse = lax.rsqrt(split_mm(mixture * mixture, mean_of) + EPSILON)
        normed = mixture * inverse
        out_ref[:, lanes(pair)] = (normed * gain).astype(BF16)
        up = u_s[:, lanes(pair)].astype(F32)
        gain_own[pl.ds(pair, 1), :] = jnp.sum(up * normed, axis=0, keepdims=True)
        grad = up * gain
        shift = split_mm(grad * normed, mean_of)
        mixed = (inverse * (grad - normed * shift)).astype(BF16)
        g_s[pair] = mixed
        qs_own[pair] = compact(mm(qet_s[pair], mixed))

    for pair in range(MINE):
        mix(MINE * core + pair)
    for swap in in_swaps:
        swap.wait_recv()
    for pair in range(MINE):
        mix(MINE * (1 - core) + pair)

    query_swaps = [to_partner(qs_own.at[MINE * (1 - core) + pair], qs_oth.at[pair], 9 + i) for i, pair in enumerate(far_pairs)]
    gain_swap = to_partner(gain_own, gain_oth, 13)
    for swap in query_swaps:
        swap.start()
    gain_swap.start()
    for pair, swap in zip(far_pairs, query_swaps):
        swap.wait_recv()
        s_0, s_1 = in_order(qs_own[MINE * core + pair], qs_oth[pair])
        c_0, _ = carries(pair)
        send3[pl.ds(pair * 4, 4)] = (s_0 + c_0 * s_1).reshape(4, ROWS, LANES)
        start_slices(2, pair, send3, recv3)
    recv3[z] = send3[z]

    places = (lax.rem(dp, 4), dp // 4, lax.rem(z, 4), group)

    def gain_copies(level, arriving):
        copies = []
        for step in range(1, 4):
            if level == 0:
                target = {"dp": row_peer(dp, step)}
            elif level == 1:
                target = {"dp": column_peer(dp, step)}
            elif level == 2:
                target = {"seq": chip(group * 4 + lax.rem(z + step, 4))}
            else:
                target = {"seq": chip(lax.rem(z + 4 * step, CHIPS))}
            there = lax.rem(places[level] + step, 4)
            slot = there if arriving else places[level]
            copies.append(
                pltpu.make_async_remote_copy(
                    gain_out.at[level], gain_in.at[level, slot], g_send.at[level, there], g_recv.at[level, slot],
                    device_id=target, device_id_type=MESH,
                )
            )
        return copies

    def send_gain(level, value):
        gain_out[level] = value
        gain_in[level, places[level]] = value
        for copy in gain_copies(level, False):
            copy.start()

    def gain_arrived(level):
        for copy in gain_copies(level, True):
            copy.wait_recv()
        return jnp.sum(gain_in[level], axis=0)

    gain_swap.wait_recv()
    send_gain(0, gain_own[...] + gain_oth[...])

    head_i = lax.broadcasted_iota(jnp.int32, (LANES, HEADS), 1)
    half_i = (lax.broadcasted_iota(jnp.int32, (LANES, HEADS), 0) >= HALF).astype(jnp.int32)
    column_i = lax.broadcasted_iota(jnp.int32, (TOK, HEADS), 1)

    def head_of(pair):
        return (head_i == 2 * pair + half_i).astype(BF16)

    later = jnp.zeros((TOK, HEADS), F32)
    for pair in range(PAIRS):
        if pair == MINE:
            send_gain(1, gain_arrived(0))
        q, k, v = q_s[:, lanes(pair)], k_s[:, lanes(pair)], v_s[:, lanes(pair)]
        mixed = g_s[pair]
        pairs = mm_t(stack(mixed), v)
        grad_weights = (pairs * p_s[pair]).astype(BF16)
        k_2 = stack(k)
        query_state = block_diagonal(si_s[pair]).astype(BF16)
        dq = mm(grad_weights[:TOK], k_2[:TOK]) + mm(grad_weights[TOK:], k_2[TOK:]) + entry_s[pair] * mm_t(mixed, query_state)
        dq_ref[:, lanes(pair)] = dq.astype(BF16)
        pairs_t = mm_t(stack(v), mixed)
        grad_weights_t = (pairs_t * pt_s[pair]).astype(BF16)
        q_2 = stack(q)
        dkl_s[pair] = mm(grad_weights_t[:TOK], q_2[:TOK]) + mm(grad_weights_t[TOK:], q_2[TOK:])
        weights_t = spt_s[pair].astype(BF16)
        g_2 = stack(mixed)
        dvl_s[pair] = mm(weights_t[:TOK], g_2[:TOK]) + mm(weights_t[TOK:], g_2[TOK:])
        balance = jnp.sum(sp_s[pair] * pairs - spt_s[pair] * pairs_t, axis=1, keepdims=True)
        later = later + jnp.where(column_i == 2 * pair, balance[:TOK], 0.0)
        later = later + jnp.where(column_i == 2 * pair + 1, balance[TOK:], 0.0)
        later = later + split_mm(car_s[pair] * mixed.astype(F32), head_of(pair))

    send_gain(2, gain_arrived(1))

    state = jnp.zeros((ROWS, LANES), F32)
    for there in reversed(range(CHIPS)):

        @pl.when(z != there)
        def _():
            from_chip(2, send3.at[there], recv3, there).wait_recv()

        send4[there] = state
        state = recv1[there, ROWS : ROWS + 1, :] * state + recv3[there]
    for there in range(CHIPS):

        @pl.when(z != there)
        def _():
            to_chip(3, send4.at[there], recv4, there).start()

    recv4[z] = send4[z]
    send_gain(3, gain_arrived(2))

    later_sum = split_mm_left((row_i <= col_i).astype(BF16), later)

    grad_swaps = []
    for i, pair in enumerate(near_pairs):
        wait_slices(3, pair, send4, recv4)
        index = MINE * core + pair
        _, s_1 = in_order(qs_own[index], qs_oth[pair])
        _, c_1 = carries(pair)
        arrived = recv4[pl.ds(pair * 4, 4)].reshape(HALF, LANES)
        own, other = in_order(s_1 + c_1 * arrived, arrived)
        sg_s[index] = own
        sg_x[pair] = other
        grad_swaps.append(to_partner(sg_x.at[pair], sg_s.at[index], 14 + i))
        grad_swaps[-1].start()

    earlier = jnp.zeros((TOK + 8, HEADS), F32)

    def finish(pair, earlier):
        k, v = k_s[:, lanes(pair)], v_s[:, lanes(pair)]
        state_grad = block_diagonal(sg_s[pair]).astype(BF16)
        dk_ref[:, lanes(pair)] = (dkl_s[pair] + exit_s[pair] * mm_t(v, state_grad)).astype(BF16)
        carried_value = exit_s[pair] * mm(k, state_grad)
        dv_ref[:, lanes(pair)] = (dvl_s[pair] + carried_value).astype(BF16)
        through = jnp.sum(si_s[pair] * sg_s[pair], axis=0, keepdims=True) * carr_own[pl.ds(pair, 1), :]
        terms = jnp.concatenate([carried_value * v.astype(F32), jnp.broadcast_to(through, (8, LANES))], axis=0)
        return earlier + split_mm(terms, head_of(pair))

    for pair in range(MINE):
        earlier = finish(MINE * core + pair, earlier)
    for swap in grad_swaps:
        swap.wait_recv()
    for pair in range(MINE):
        earlier = finish(MINE * (1 - core) + pair, earlier)
    total = later_sum + split_mm_left((row_i > col_i).astype(BF16), earlier[:TOK]) + earlier[TOK : TOK + 1]
    dd_ref[...] = total.T
    dg_ref[...] = gain_arrived(3)

    for swap in (carry_swap, gain_swap, *state_swaps, *in_swaps, *query_swaps, *grad_swaps):
        swap.wait_send()
    for step in range(1, CHIPS):
        there = lax.rem(z + step, CHIPS)
        to_chip(0, send1.at[there, pl.ds(0, SENT)], recv1.at[:, pl.ds(0, SENT)], there).wait_send()
        for phase, source, target in ((1, send2, recv2), (2, send3, recv3), (3, send4, recv4)):
            to_chip(phase, source.at[there], target, there).wait_send()
    for level in range(4):
        for copy in gain_copies(level, False):
            copy.wait_send()


def write_out(*refs):
    sources, targets, sem = refs[:6], refs[6:12], refs[12]
    copies = [pltpu.make_async_copy(source, target, sem.at[i]) for i, (source, target) in enumerate(zip(sources, targets))]
    for copy in copies:
        copy.start()
    for copy in copies:
        copy.wait()


def local(queries, key_vectors, value_vectors, log_decay, restart, norm_gain, upstream):
    width = queries.shape[-1]
    vmem = pl.BlockSpec(memory_space=pltpu.VMEM)
    hbm = pl.BlockSpec(memory_space=pltpu.HBM)
    wide = pltpu.VMEM((TOK, width), BF16)
    table = pltpu.VMEM((PAIRS, TOK, LANES), F32)
    table_bf16 = pltpu.VMEM((PAIRS, TOK, LANES), BF16)
    double = pltpu.VMEM((PAIRS, 2 * TOK, LANES), F32)
    states = pltpu.VMEM((PAIRS, HALF, LANES), F32)
    some_states = pltpu.VMEM((MINE, HALF, LANES), F32)
    tile = pltpu.VMEM((8, LANES), F32)
    slices = pltpu.VMEM((CHIPS, ROWS, LANES), F32)
    slices_and = pltpu.VMEM((CHIPS, ROWS + 8, LANES), F32)
    dma = pltpu.SemaphoreType.DMA
    rows = jax.ShapeDtypeStruct((TOK, width), BF16)
    results = (
        rows, rows, rows, rows,
        jax.ShapeDtypeStruct((HEADS, TOK), F32),
        jax.ShapeDtypeStruct((8, LANES), F32),
    )
    outs = pl.pallas_call(
        kernel,
        out_shape=results,
        in_specs=[hbm] * 7,
        out_specs=[vmem] * 6,
        scratch_shapes=[
            wide, wide, wide, wide,
            pltpu.VMEM((HEADS, TOK), F32), pltpu.VMEM((1, TOK), jnp.int32), tile, dma((7,)),
            table, table, double, double, double, double, table, table, table_bf16, table_bf16, table, table,
            states, some_states, states, some_states, tile, tile, states, some_states, states, some_states,
            slices_and, slices_and, slices, slices, slices, slices, slices, slices,
            tile, tile, pltpu.VMEM((4, 8, LANES), F32), pltpu.VMEM((4, 4, 8, LANES), F32),
            dma((18,)), dma((18,)), dma((4, CHIPS)), dma((4, CHIPS)), dma((4, 4)), dma((4, 4)),
        ],
        compiler_params=pltpu.CompilerParams(collective_id=0, has_side_effects=True, vmem_limit_bytes=32 * 1024 * 1024),
    )(
        *(
            pltpu.with_memory_space_constraint(array, pltpu.HBM)
            for array in (
                queries[0], key_vectors[0], value_vectors[0], upstream[0],
                log_decay[0].T, restart, norm_gain.reshape(8, LANES),
            )
        )
    )
    layer_out, dq, dk, dv, dd, dg = pl.pallas_call(
        write_out,
        out_shape=tuple(pltpu.HBM(result.shape, result.dtype) for result in results),
        in_specs=[vmem] * 6,
        out_specs=[hbm] * 6,
        scratch_shapes=[dma((6,))],
    )(*(pltpu.with_memory_space_constraint(array, pltpu.VMEM) for array in outs))
    return (layer_out[None], dq[None], dk[None], dv[None], dd.T[None], dg.reshape(-1))


def solution(mesh):
    row, narrow = P("dp", "seq", None), P("dp", "seq")
    return jax.shard_map(
        local,
        mesh=mesh,
        in_specs=(row, row, row, row, narrow, P(), row),
        out_specs=(row, row, row, row, row, P()),
        check_vma=False,
    )
```

time: 77.2 us -> 62.9 us (0.81)
  local copies, waits for them, and re-layouts: 9.31 us -> 0 us
  Pallas kernels: 66.2 us -> 61.8 us
    unnamed x21 -> x0, local copies, waits for them, and re-layouts: 9.31 us -> none
    pallas_call x1 -> x2, Pallas kernels: 66.2 us -> 61.8 us  [the longest x1 60.7 us: local(): pl.pallas_call(kernel, out_shape=results, in_specs=[hbm] * 7, out_specs=[...]
where the time goes in v2:
time: 62.9 us; the launch traced here: 62.4 us
  Pallas kernels  61.8 us (98%)
  between operations  0.64 us (1%)
    pallas_call x1, Pallas kernels, local(): pl.pallas_call(kernel, out_shape=results, in_specs=[hbm] * 7, out_specs=[...  60.7 us

profile of v2, /device:TPU:1, one launch (start us, length us, event | category | flops | bytes accessed | tf_op | source)
XLA Modules:
  0.0 62.4 jit_solution(2404924602505019955)
XLA Ops:
  0.6 60.7 %shard_map.118 = (bf16[128,1024]{1,0:T(8,128)(2,1)S(1)}, bf16[128,1024]{1,0:T(8,128)(2,1)S(1)}, bf16[128,1024]{1,0:T(8,128)(2,1)S(1)}, bf16[128,1024]{1,0:T(8,12...) custom-call(bf16[128,1024]{1,0:T(8,128)(2,1)} %bitcast.16, bf16[128,1024]{1,0:T(8,128)(2,1)} %bitcast.17, ...), custom_call_target="tpu_custom_call" | custom-call | tf_op jit(solution)/shard_map/pallas_call | solution.py:469
  61.4 1.0 %shard_map.119 = (bf16[128,1024]{1,0:T(8,128)(2,1)}, bf16[128,1024]{1,0:T(8,128)(2,1)}, bf16[128,1024]{1,0:T(8,128)(2,1)}, bf16[128,1024]{1,0:T(8,128)(2,1)}, f32[16,128]{1,0:T(8,128)}, /*index=5*/f32[8,128]{1,0:T(8,128)}) custom-call(bf16[128,1024]{1,0:T(8,128)(2,1)S(1)} %get-tuple-element.18.refs_0_, bf16[128,1024]{1,0:T(8,128)(2,1)S(1)} %get-tuple-element.19.refs_1_, ...), custom_call_target="tpu_custom_call" | custom-call | tf_op jit(solution)/shard_map/pallas_call | solution.py:493

commit v3 on v2

--- a/solution.py
+++ b/solution.py
@@ -74,14 +74,6 @@
     def chip(index):
         return index * 2 + core
 
-    barrier = pltpu.get_barrier_semaphore()
-    for step in FAR_FIRST:
-        pl.semaphore_signal(barrier, inc=1, device_id={"seq": chip(lax.rem(z + step, CHIPS))}, device_id_type=MESH)
-    for step in range(1, 4):
-        for there in (row_peer(dp, step), column_peer(dp, step)):
-            pl.semaphore_signal(barrier, inc=1, device_id={"dp": there}, device_id_type=MESH)
-    pl.semaphore_signal(barrier, inc=1, device_id={"seq": partner}, device_id_type=MESH)
-
     loads = [
         pltpu.make_async_copy(source, target, in_sem.at[i])
         for i, (source, target) in enumerate(
@@ -90,6 +82,14 @@
     ]
     for load in loads:
         load.start()
+
+    barrier = pltpu.get_barrier_semaphore()
+    for step in FAR_FIRST:
+        pl.semaphore_signal(barrier, inc=1, device_id={"seq": chip(lax.rem(z + step, CHIPS))}, device_id_type=MESH)
+    for step in range(1, 4):
+        for there in (row_peer(dp, step), column_peer(dp, step)):
+            pl.semaphore_signal(barrier, inc=1, device_id={"dp": there}, device_id_type=MESH)
+    pl.semaphore_signal(barrier, inc=1, device_id={"seq": partner}, device_id_type=MESH)
 
     def lanes(pair):
         if isinstance(pair, int):
@@ -179,11 +179,13 @@
         index = pl.ds(MINE * core + pair, 1)
         return in_order(carr_own[index, :], carr_oth[index, :])
 
+    unsent = (CHIPS - 1, 0, 0, CHIPS - 1)
+
     def start_slices(phase, pair, source, target):
         for i in range(4):
             there = pair * 4 + i
 
-            @pl.when(there != z)
+            @pl.when((there != z) & (z != unsent[phase]))
             def _():
                 to_chip(phase, source.at[there], target, there).start()
 
@@ -221,20 +223,28 @@
         loc_s[pair] = mm(weights[:TOK], v_2[:TOK]) + mm(weights[TOK:], v_2[TOK:])
 
     state = jnp.zeros((ROWS, LANES), F32)
-    for there in range(CHIPS):
+    for there in range(CHIPS - 1):
 
         @pl.when(z != there)
         def _():
             from_chip(0, send1.at[there, pl.ds(0, SENT)], recv1.at[:, pl.ds(0, SENT)], there).wait_recv()
 
-        send2[there] = state
-
-        @pl.when(z != there)
+        state = recv1[there, ROWS : ROWS + 1, :] * state + recv1[there, :ROWS, :]
+        send2[there + 1] = state
+    for step in FAR_FIRST:
+        there = lax.rem(z + step, CHIPS)
+
+        @pl.when(there != 0)
         def _():
             to_chip(1, send2.at[there], recv2, there).start()
 
-        state = recv1[there, ROWS : ROWS + 1, :] * state + recv1[there, :ROWS, :]
-    recv2[z] = send2[z]
+    @pl.when(z != 0)
+    def _():
+        recv2[z] = send2[z]
+
+    @pl.when(z == 0)
+    def _():
+        recv2[...] = jnp.zeros_like(recv2)
 
     for pair in range(PAIRS):
         q, k = q_s[:, lanes(pair)], k_s[:, lanes(pair)]
@@ -245,7 +255,7 @@
         for i in range(4):
             there = pair * 4 + i
 
-            @pl.when(there != z)
+            @pl.when((there != z) & (z != unsent[phase]))
             def _():
                 from_chip(phase, source.at[there], target, there).wait_recv()
 
@@ -269,14 +279,15 @@
         carried = entry_s[pair] * mm(q, block_diagonal(si_s[pair]).astype(BF16))
         car_s[pair] = carried
         mixture = loc_s[pair] + carried
-        inverse = lax.rsqrt(split_mm(mixture * mixture, mean_of) + EPSILON)
+        up = u_s[:, lanes(pair)].astype(F32)
+        grad = up * gain
+        square = split_mm(mixture * mixture, mean_of)
+        product = split_mm(grad * mixture, mean_of)
+        inverse = lax.rsqrt(square + EPSILON)
         normed = mixture * inverse
+        mixed = (inverse * (grad - normed * (inverse * product))).astype(BF16)
         out_ref[:, lanes(pair)] = (normed * gain).astype(BF16)
-        up = u_s[:, lanes(pair)].astype(F32)
         gain_own[pl.ds(pair, 1), :] = jnp.sum(up * normed, axis=0, keepdims=True)
-        grad = up * gain
-        shift = split_mm(grad * normed, mean_of)
-        mixed = (inverse * (grad - normed * shift)).astype(BF16)
         g_s[pair] = mixed
         qs_own[pair] = compact(mm(qet_s[pair], mixed))
 
@@ -371,21 +382,28 @@
     send_gain(2, gain_arrived(1))
 
     state = jnp.zeros((ROWS, LANES), F32)
-    for there in reversed(range(CHIPS)):
+    for there in reversed(range(1, CHIPS)):
 
         @pl.when(z != there)
         def _():
             from_chip(2, send3.at[there], recv3, there).wait_recv()
 
-        send4[there] = state
-        state = recv1[there, ROWS : ROWS + 1, :] * state + recv3[there]
-    for there in range(CHIPS):
+        state = recv3[there] if there == CHIPS - 1 else recv1[there, ROWS : ROWS + 1, :] * state + recv3[there]
+        send4[there - 1] = state
+    for there in range(CHIPS - 1):
 
         @pl.when(z != there)
         def _():
             to_chip(3, send4.at[there], recv4, there).start()
 
-    recv4[z] = send4[z]
+    @pl.when(z != CHIPS - 1)
+    def _():
+        recv4[z] = send4[z]
+
+    @pl.when(z == CHIPS - 1)
+    def _():
+        recv4[...] = jnp.zeros_like(recv4)
+
     send_gain(3, gain_arrived(2))
 
     later_sum = split_mm_left((row_i <= col_i).astype(BF16), later)
@@ -429,9 +447,18 @@
         swap.wait_send()
     for step in range(1, CHIPS):
         there = lax.rem(z + step, CHIPS)
-        to_chip(0, send1.at[there, pl.ds(0, SENT)], recv1.at[:, pl.ds(0, SENT)], there).wait_send()
-        for phase, source, target in ((1, send2, recv2), (2, send3, recv3), (3, send4, recv4)):
-            to_chip(phase, source.at[there], target, there).wait_send()
+        copies = (
+            to_chip(0, send1.at[there, pl.ds(0, SENT)], recv1.at[:, pl.ds(0, SENT)], there),
+            to_chip(1, send2.at[there], recv2, there),
+            to_chip(2, send3.at[there], recv3, there),
+            to_chip(3, send4.at[there], recv4, there),
+        )
+        for phase, copy in enumerate(copies):
+
+            @pl.when((there if phase % 2 else z) != unsent[phase])
+            def _(copy=copy):
+                copy.wait_send()
+
     for level in range(4):
         for copy in gain_copies(level, False):
             copy.wait_send()

time: 62.9 us -> 60 us (0.954)
  Pallas kernels: 61.8 us -> 59.2 us
    pallas_call x1, Pallas kernels: 60.7 us -> 58.2 us  [local(): pl.pallas_call(kernel, out_shape=results, in_specs=[hbm] * 7, out_specs=[...]
where the time goes in v3:
time: 60 us; the launch traced here: 59.9 us
  Pallas kernels  59.2 us (99%)
  between operations  0.64 us (1%)
    pallas_call x1, Pallas kernels, local(): pl.pallas_call(kernel, out_shape=results, in_specs=[hbm] * 7, out_specs=[...  58.2 us

profile of v3, /device:TPU:1, one launch (start us, length us, event | category | flops | bytes accessed | tf_op | source)
XLA Modules:
  0.0 59.9 jit_solution(14707116833143990551)
XLA Ops:
  0.6 58.2 %shard_map.118 = (bf16[128,1024]{1,0:T(8,128)(2,1)S(1)}, bf16[128,1024]{1,0:T(8,128)(2,1)S(1)}, bf16[128,1024]{1,0:T(8,128)(2,1)S(1)}, bf16[128,1024]{1,0:T(8,12...) custom-call(bf16[128,1024]{1,0:T(8,128)(2,1)} %bitcast.16, bf16[128,1024]{1,0:T(8,128)(2,1)} %bitcast.17, ...), custom_call_target="tpu_custom_call" | custom-call | tf_op jit(solution)/shard_map/pallas_call | solution.py:496
  58.9 1.0 %shard_map.119 = (bf16[128,1024]{1,0:T(8,128)(2,1)}, bf16[128,1024]{1,0:T(8,128)(2,1)}, bf16[128,1024]{1,0:T(8,128)(2,1)}, bf16[128,1024]{1,0:T(8,128)(2,1)}, f32[16,128]{1,0:T(8,128)}, /*index=5*/f32[8,128]{1,0:T(8,128)}) custom-call(bf16[128,1024]{1,0:T(8,128)(2,1)S(1)} %get-tuple-element.18.refs_0_, bf16[128,1024]{1,0:T(8,128)(2,1)S(1)} %get-tuple-element.19.refs_1_, ...), custom_call_target="tpu_custom_call" | custom-call | tf_op jit(solution)/shard_map/pallas_call | solution.py:520

commit v4 on v3

--- a/solution.py
+++ b/solution.py
@@ -41,6 +41,12 @@
     return mm(high, b) + mm(low, b)
 
 
+def split_t_mm(a, b):
+    high = a.astype(BF16)
+    low = (a - high.astype(F32)).astype(BF16)
+    return t_mm(high, b) + t_mm(low, b)
+
+
 def split_mm_left(a, b):
     high = b.astype(BF16)
     low = (b - high.astype(F32)).astype(BF16)
@@ -59,7 +65,7 @@
     q_hbm, k_hbm, v_hbm, u_hbm, ld_hbm, rs_hbm, gain_hbm,
     out_ref, dq_ref, dk_ref, dv_ref, dd_ref, dg_ref,
     q_s, k_s, v_s, u_s, ld_ref, rs_ref, gain_ref, in_sem,
-    entry_s, exit_s, p_s, pt_s, sp_s, spt_s, loc_s, car_s, qet_s, g_s, dkl_s, dvl_s,
+    entry_s, exit_s, p_s, pt_s, sp_s, spt_s, loc_s, car_s, qet_s, qetl_s, g_s, dkl_s, dvl_s,
     st_own, st_oth, qs_own, qs_oth, carr_own, carr_oth, si_s, si_x, sg_s, sg_x,
     send1, recv1, send2, recv2, send3, recv3, send4, recv4,
     gain_own, gain_oth, gain_out, gain_in,
@@ -137,8 +143,8 @@
     loads[2].wait()
     loads[3].wait()
     for pair in range(PAIRS):
-        decayed = (k_s[:, lanes(pair)].astype(F32) * exit_s[pair]).astype(BF16)
-        st_own[pair] = compact(t_mm(decayed, v_s[:, lanes(pair)]))
+        decayed = k_s[:, lanes(pair)].astype(F32) * exit_s[pair]
+        st_own[pair] = compact(split_t_mm(decayed, v_s[:, lanes(pair)]))
 
     pl.semaphore_wait(barrier, 22)
 
@@ -222,6 +228,13 @@
         v_2 = stack(v)
         loc_s[pair] = mm(weights[:TOK], v_2[:TOK]) + mm(weights[TOK:], v_2[TOK:])
 
+    for pair in range(PAIRS):
+        q, k = q_s[:, lanes(pair)], k_s[:, lanes(pair)]
+        spt_s[pair] = mm_t(stack(k), q) * pt_s[pair]
+        decayed = (q.astype(F32) * entry_s[pair]).T
+        qet_s[pair] = decayed.astype(BF16)
+        qetl_s[pair] = (decayed - decayed.astype(BF16).astype(F32)).astype(BF16)
+
     state = jnp.zeros((ROWS, LANES), F32)
     for there in range(CHIPS - 1):
 
@@ -245,11 +258,6 @@
     @pl.when(z == 0)
     def _():
         recv2[...] = jnp.zeros_like(recv2)
-
-    for pair in range(PAIRS):
-        q, k = q_s[:, lanes(pair)], k_s[:, lanes(pair)]
-        spt_s[pair] = mm_t(stack(k), q) * pt_s[pair]
-        qet_s[pair] = (q.astype(F32) * entry_s[pair]).T.astype(BF16)
 
     def wait_slices(phase, pair, source, target):
         for i in range(4):
@@ -276,7 +284,7 @@
     def mix(pair):
         q = q_s[:, lanes(pair)]
         gain = gain_ref[pl.ds(pair, 1), :]
-        carried = entry_s[pair] * mm(q, block_diagonal(si_s[pair]).astype(BF16))
+        carried = entry_s[pair] * split_mm_left(q, block_diagonal(si_s[pair]))
         car_s[pair] = carried
         mixture = loc_s[pair] + carried
         up = u_s[:, lanes(pair)].astype(F32)
@@ -289,7 +297,7 @@
         out_ref[:, lanes(pair)] = (normed * gain).astype(BF16)
         gain_own[pl.ds(pair, 1), :] = jnp.sum(up * normed, axis=0, keepdims=True)
         g_s[pair] = mixed
-        qs_own[pair] = compact(mm(qet_s[pair], mixed))
+        qs_own[pair] = compact(mm(qet_s[pair], mixed) + mm(qetl_s[pair], mixed))
 
     for pair in range(MINE):
         mix(MINE * core + pair)
@@ -425,9 +433,9 @@
 
     def finish(pair, earlier):
         k, v = k_s[:, lanes(pair)], v_s[:, lanes(pair)]
-        state_grad = block_diagonal(sg_s[pair]).astype(BF16)
-        dk_ref[:, lanes(pair)] = (dkl_s[pair] + exit_s[pair] * mm_t(v, state_grad)).astype(BF16)
-        carried_value = exit_s[pair] * mm(k, state_grad)
+        state_grad = block_diagonal(sg_s[pair])
+        dk_ref[:, lanes(pair)] = (dkl_s[pair] + exit_s[pair] * mm_t(v, state_grad.astype(BF16))).astype(BF16)
+        carried_value = exit_s[pair] * split_mm_left(k, state_grad)
         dv_ref[:, lanes(pair)] = (dvl_s[pair] + carried_value).astype(BF16)
         through = jnp.sum(si_s[pair] * sg_s[pair], axis=0, keepdims=True) * carr_own[pl.ds(pair, 1), :]
         terms = jnp.concatenate([carried_value * v.astype(F32), jnp.broadcast_to(through, (8, LANES))], axis=0)
@@ -501,7 +509,7 @@
         scratch_shapes=[
             wide, wide, wide, wide,
             pltpu.VMEM((HEADS, TOK), F32), pltpu.VMEM((1, TOK), jnp.int32), tile, dma((7,)),
-            table, table, double, double, double, double, table, table, table_bf16, table_bf16, table, table,
+            table, table, double, double, double, double, table, table, table_bf16, table_bf16, table_bf16, table, table,
             states, some_states, states, some_states, tile, tile, states, some_states, states, some_states,
             slices_and, slices_and, slices, slices, slices, slices, slices, slices,
             tile, tile, pltpu.VMEM((4, 8, LANES), F32), pltpu.VMEM((4, 4, 8, LANES), F32),

time: 60 us -> 60.2 us (level)
  no operation moved by 1% of the time
where the time goes in v4:
time: 60.2 us; the launch traced here: 60.1 us
  Pallas kernels  59.4 us (99%)
  between operations  0.64 us (1%)
    pallas_call x1, Pallas kernels, local(): pl.pallas_call(kernel, out_shape=results, in_specs=[hbm] * 7, out_specs=[...  58.4 us

profile of v4, /device:TPU:1, one launch (start us, length us, event | category | flops | bytes accessed | tf_op | source)
XLA Modules:
  0.0 60.1 jit_solution(11387586784131138014)
XLA Ops:
  0.6 58.4 %shard_map.118 = (bf16[128,1024]{1,0:T(8,128)(2,1)S(1)}, bf16[128,1024]{1,0:T(8,128)(2,1)S(1)}, bf16[128,1024]{1,0:T(8,128)(2,1)S(1)}, bf16[128,1024]{1,0:T(8,12...) custom-call(bf16[128,1024]{1,0:T(8,128)(2,1)} %bitcast.16, bf16[128,1024]{1,0:T(8,128)(2,1)} %bitcast.17, ...), custom_call_target="tpu_custom_call" | custom-call | tf_op jit(solution)/shard_map/pallas_call | solution.py:504
  59.0 1.0 %shard_map.119 = (bf16[128,1024]{1,0:T(8,128)(2,1)}, bf16[128,1024]{1,0:T(8,128)(2,1)}, bf16[128,1024]{1,0:T(8,128)(2,1)}, bf16[128,1024]{1,0:T(8,128)(2,1)}, f32[16,128]{1,0:T(8,128)}, /*index=5*/f32[8,128]{1,0:T(8,128)}) custom-call(bf16[128,1024]{1,0:T(8,128)(2,1)S(1)} %get-tuple-element.18.refs_0_, bf16[128,1024]{1,0:T(8,128)(2,1)S(1)} %get-tuple-element.19.refs_1_, ...), custom_call_target="tpu_custom_call" | custom-call | tf_op jit(solution)/shard_map/pallas_call | solution.py:528

commit v5 on v4

--- a/solution.py
+++ b/solution.py
@@ -398,7 +398,7 @@
 
         state = recv3[there] if there == CHIPS - 1 else recv1[there, ROWS : ROWS + 1, :] * state + recv3[there]
         send4[there - 1] = state
-    for there in range(CHIPS - 1):
+    for there in (1, 0, 2, 3, 4, 5, 6, 7, 14, 13, 12, 11, 10, 9, 8):
 
         @pl.when(z != there)
         def _():

time: 60.2 us -> 61.3 us (1.018)
  Pallas kernels: 59.4 us -> 60.5 us
    pallas_call x1, Pallas kernels: 58.4 us -> 59.5 us  [local(): pl.pallas_call(kernel, out_shape=results, in_specs=[hbm] * 7, out_specs=[...]
where the time goes in v5:
time: 61.3 us; the launch traced here: 61.2 us
  Pallas kernels  60.5 us (99%)
  between operations  0.64 us (1%)
    pallas_call x1, Pallas kernels, local(): pl.pallas_call(kernel, out_shape=results, in_specs=[hbm] * 7, out_specs=[...  59.5 us

profile of v5, /device:TPU:1, one launch (start us, length us, event | category | flops | bytes accessed | tf_op | source)
XLA Modules:
  0.0 61.2 jit_solution(10759874412412259413)
XLA Ops:
  0.6 59.5 %shard_map.118 = (bf16[128,1024]{1,0:T(8,128)(2,1)S(1)}, bf16[128,1024]{1,0:T(8,128)(2,1)S(1)}, bf16[128,1024]{1,0:T(8,128)(2,1)S(1)}, bf16[128,1024]{1,0:T(8,12...) custom-call(bf16[128,1024]{1,0:T(8,128)(2,1)} %bitcast.16, bf16[128,1024]{1,0:T(8,128)(2,1)} %bitcast.17, ...), custom_call_target="tpu_custom_call" | custom-call | tf_op jit(solution)/shard_map/pallas_call | solution.py:504
  60.2 1.0 %shard_map.119 = (bf16[128,1024]{1,0:T(8,128)(2,1)}, bf16[128,1024]{1,0:T(8,128)(2,1)}, bf16[128,1024]{1,0:T(8,128)(2,1)}, bf16[128,1024]{1,0:T(8,128)(2,1)}, f32[16,128]{1,0:T(8,128)}, /*index=5*/f32[8,128]{1,0:T(8,128)}) custom-call(bf16[128,1024]{1,0:T(8,128)(2,1)S(1)} %get-tuple-element.18.refs_0_, bf16[128,1024]{1,0:T(8,128)(2,1)S(1)} %get-tuple-element.19.refs_1_, ...), custom_call_target="tpu_custom_call" | custom-call | tf_op jit(solution)/shard_map/pallas_call | solution.py:528
